TPU v7x, 32 devices: a whole 2x2x4 slice. The times are simulated.
32 devices in a mesh: batch: 4 (over z), seq: 8 (over y, x, core).
Axes of the slice: x: 2, y: 2, z: 4, core: 2. Of those that a mesh axis runs over, the one named last changes fastest.
Arguments:
- queries: bfloat16 [16384, 8, 256], P(('batch', 'seq')), parts along dimension 0, may hold values from -400 to 400
- key_heads: bfloat16 [16384, 4, 256], P(('batch', 'seq')), parts along dimension 0, may hold values from -16 to 16
- projected_value_heads: bfloat16 [16384, 4, 256], P(('batch', 'seq')), parts along dimension 0, may hold values from -6 to 6
- lengths: int32 [4], P('batch'), parts along dimension 0, may hold values from 3585 to 4096
Outputs:
- attended: bfloat16 [16384, 8, 256], P(('batch', 'seq')), parts along dimension 0
There are 4 independent parts, one for each index of `batch`. A program takes and returns all parts, laid end to end along the dimension named above; each array names one. Nothing has to cross between parts.
All inputs are finite; a program needn't handle non-finite values.
Results may differ from a plain program's by a relative error of at most 0.0033.
Values may be sent and summed in bfloat16 or wider, within the bound.
No kernel may reach another device: no remote copies, remote signals or barrier semaphores. Data moves between devices by JAX's collectives and lax.ppermute only.
A program may use at most 192 MiB of HBM per device.

v0:
```python
import math
import jax
import jax.numpy as jnp
from jax import lax
from jax.sharding import PartitionSpec as P

WINDOW = 4096
SINKS = 4


def spread(value, axis, source):
    kept = jnp.where(lax.axis_index(axis) == source, value, 0).astype(value.dtype)
    return lax.psum(kept, axis)


def shards(queries, key_heads, projected_value_heads, lengths):
    tok_rows = queries.shape[0]
    head_count = queries.shape[1]
    head_width = queries.shape[2]
    kv_heads = key_heads.shape[1]
    share = head_count // kv_heads
    position = lax.axis_index("seq")
    length_now = lengths[0]
    first_row = position * tok_rows
    score_scale = head_width ** (-0.5)
    grouped = queries.reshape(tok_rows, kv_heads, share, head_width)
    query_pos = first_row + jnp.arange(tok_rows, dtype=jnp.int32)
    last_query = first_row + tok_rows - 1

    def attend(running, kv_block, key_start, sink_mode):
        key_count = kv_block.shape[1]
        key_pos = key_start + jnp.arange(key_count, dtype=jnp.int32)
        if sink_mode:
            useful = first_row < length_now
        else:
            useful = (
                (key_start <= last_query)
                & (key_start + key_count - 1 > first_row - WINDOW)
                & (key_start < length_now)
                & (first_row < length_now)
                & (key_start + key_count > SINKS)
            )

        def compute(current):
            maximum, totals, weighted = current
            scores = (
                jnp.einsum(
                    "qhgd,khd->hgqk", grouped, kv_block[0], preferred_element_type=jnp.float32
                )
                * score_scale
            )
            distance = query_pos[:, None] - key_pos[None, :]
            if sink_mode:
                visible = (distance >= 0) & (key_pos[None, :] < length_now)
            else:
                visible = (
                    (distance >= 0)
                    & (distance < WINDOW)
                    & (key_pos[None, :] >= SINKS)
                    & (key_pos[None, :] < length_now)
                )
            visible = visible & (query_pos[:, None] < length_now)
            masked = jnp.where(visible, scores, -1e30)
            newest = jnp.maximum(maximum, jnp.max(masked, axis=-1))
            weights = jnp.where(visible, jnp.exp(scores - newest[..., None]), 0.0)
            rescale = jnp.exp(maximum - newest)
            totals = totals * rescale + jnp.sum(weights, axis=-1)
            weighted = weighted * rescale[..., None] + jnp.einsum(
                "hgqk,khd->hgqd",
                weights.astype(jnp.bfloat16),
                kv_block[1],
                preferred_element_type=jnp.float32,
            )
            return (newest, totals, weighted)

        return lax.cond(useful, compute, lambda current: current, running)

    running = (
        jnp.full((kv_heads, share, tok_rows), -1e30, jnp.float32),
        jnp.zeros((kv_heads, share, tok_rows), jnp.float32),
        jnp.zeros((kv_heads, share, tok_rows, head_width), jnp.float32),
    )
    own_pair = jnp.stack([key_heads, projected_value_heads])
    sink_pair = spread(own_pair[:, :SINKS], "seq", 0)
    running = attend(running, sink_pair, jnp.int32(0), True)
    shard_piece = lax.all_gather(own_pair, "seq", axis=1, tiled=True)
    piece_rows = shard_piece.shape[1]
    block_size = math.gcd(piece_rows, tok_rows)

    def one_slice(slice_index, inner):
        sliced = lax.dynamic_slice_in_dim(shard_piece, slice_index * block_size, block_size, 1)
        return attend(inner, sliced, slice_index * block_size, False)

    running = lax.fori_loop(0, piece_rows // block_size, one_slice, running)
    maximum, totals, weighted = running
    valid = query_pos < length_now
    result = jnp.where(valid[:, None], weighted / jnp.where(valid, totals, 1.0)[..., None], 0.0)
    return (
        result.transpose(2, 0, 1, 3).reshape(tok_rows, head_count, head_width).astype(jnp.bfloat16)
    )


def solution(mesh):
    in_specs = (
        P(("batch", "seq"), None, None),
        P(("batch", "seq"), None, None),
        P(("batch", "seq"), None, None),
        P("batch"),
    )
    out_specs = P(("batch", "seq"), None, None)
    return jax.shard_map(shards, mesh=mesh, in_specs=in_specs, out_specs=out_specs, check_vma=False)
```

profile of v0, /device:TPU:7, one launch (start us, length us, event | category | flops | bytes accessed | tf_op | source)
XLA Modules:
  0.0 233.9 jit_solution(17987228410753566416)
XLA Ops:
  6.5 1.8 copy_bitcast_fusion
  8.4 1.5 pad_maximum_fusion
  10.5 3.3 %copy.8 = bf16[512,8,256]{2,0,1:T(8,128)(2,1)} copy(bf16[512,8,256]{2,1,0:T(8,128)(2,1)} %param.10) | data formatting | bytes 4194304 | tf_op args[0]
  13.9 23.0 %psum.7 = bf16[2,4,4,256]{3,1,2,0:T(4,128)(2,1)S(1)} all-reduce(bf16[2,4,4,256]{3,1,2,0:T(4,128)(2,1)S(1)} %fusion.40), channel_id=1, replica_groups=mesh['batch'=4,'seq'=8] {'seq'}, use_global_device_ids=true, to_apply=%region_0.1 | all-reduce | flops 8192 | bytes 32768 | tf_op jit(solution)/shard_map/psum | solution.py:13
  36.9 9.0 %conditional.2 = (f32[4,2,512]{2,1,0:T(2,128)}, f32[4,2,512]{2,1,0:T(2,128)S(1)}, f32[4,2,512,256]{3,2,1,0:T(8,128)}) conditional(s32[]{:T(128)} %convert_element_type.35, () %tuple.61, (s32[512]{0:T(512)S(1)}, s32[4]{0:T(128)S(1)}, s32[]{:T(128)}, s32[4]{0:T(128)S(1)}, bf16[2,4,4,256]{3,1,2,0:T(4,128)(2,1)S(1)}, ...), branch_computations={%region_1.2_spmd, %region_2.5_spmd} | conditional | flops 17998340 | bytes 6698056 | solution.py:76
  38.3 2.3 select_reduce_fusion
  41.2 0.8 fusion.4
  42.0 0.7 fusion.16
  42.8 3.2 %convolution_add_fusion = f32[4,2,512,256]{3,2,1,0:T(8,128)} fusion(f32[4,2,512]{2,1,0:T(2,128)S(1)} %get-tuple-element.538, f32[4,2,512,4]{2,3,1,0:T(4,128)S(1)} %get-tuple-element.547, f32[4,2,512]{2,1,0:T(2,128)} %get-tuple-element.637, pred[512,4]{0,1:T(4,128)(4,1)S(1)} %fusion.14, bf16[2,4,4,256]{3,1,2,0:T(4,128)(2,1)S(1)} %get-tuple-element.449), kind=kOutput, calls=%fused_computation.1 | convolution fusion | flops 9486336 | bytes 4302848 | tf_op jit(solution)/shard_map/cond/branch_1_fun/hgqk,khd->hgqd/dot_general | solution.py:68
  46.0 54.7 %all-gather.2.cloned.1.call-done = bf16[2,4096,4,256]{3,1,2,0:T(8,128)(2,1)} async-done(((bf16[2,512,4,256]{3,1,2,0:T(8,128)(2,1)}), bf16[2,4096,4,256]{3,1,2,0:T(8,128)(2,1)}) %all-gather.2.cloned.1.call-update) | async-done | bytes 16777232 | tf_op jit(solution)/shard_map/all_gather | solution.py:86
  100.6 121.3 %while.22 = (s32[]{:T(128)}, f32[4,2,512]{2,1,0:T(2,128)}, f32[4,2,512]{2,1,0:T(2,128)S(1)}, f32[4,2,512,256]{3,2,1,0:T(8,128)}, s32[]{:T(128)}, /*index=5*/s32[...) while((s32[]{:T(128)}, f32[4,2,512]{2,1,0:T(2,128)}, ...), condition=%wide.region_10.11_spmd.clone, body=%wide.region_5.10_spmd.clone.sunk | while | flops 2174495232 | bytes 39079348 | solution.py:94
  101.3 14.5 %conditional.5 = ((f32[4,2,512]{2,1,0:T(2,128)}, f32[4,2,512]{2,1,0:T(2,128)S(1)}, f32[4,2,512,256]{3,2,1,0:T(8,128)})) conditional(s32[]{:T(128)} %convert_element_type.48, (f32[4,2,512]{2,1,0:T(2,128)}, f32[4,2,512]{2,1,0:T(2,128)S(1)}, f32[4,2,512,256]{3,2,1,0:T(8,128)}) %tuple.88, (s32[]{:T(128)}, s32[]{:T(128)}, s32[512]{0:T(512)S(1)}, ...), branch_computations={%region_6.6_spmd, %region_7.9_spmd} | conditional | flops 2174495232 | bytes 39076968 | solution.py:76
  102.4 3.5 %fusion.17 = (f32[4,2,512]{2,1,0:T(2,128)S(1)}, f32[4,512,512,2]{2,1,3,0:T(8,128)S(1)}) fusion(pred[512,512]{0,1:T(8,128)(4,1)S(1)} %fusion.34, bf16[512,4,2,256]{3,0,2,1:T(8,128)(2,1)} %get-tuple-element.457, bf16[2,4096,4,256]{3,1,2,0:T(8,128)(2,1)} %get-tuple-element.456, s32[]{:T(128)S(6)} %select_n.38), kind=kOutput, calls=%fused_computation.26 | convolution fusion | flops 1080029184 | bytes 11812868 | tf_op jit(solution)/shard_map/while/body/eval_jaxpr/cond/branch_1_fun/qhgd,khd->hgqk/dot_general | solution.py:47
  106.6 1.7 fusion.21
  109.1 6.1 %multiply_add_fusion = f32[4,2,512,256]{3,2,1,0:T(8,128)} fusion(f32[4,2,512,256]{3,2,1,0:T(8,128)} %get-tuple-element.459, f32[4,2,512]{2,1,0:T(2,128)S(1)} %bitcast.69, f32[4,512,512,2]{2,1,3,0:T(8,128)S(1)} %get-tuple-element.549, f32[4,2,512]{2,1,0:T(2,128)S(1)} %max.4, pred[512,512]{0,1:T(8,128)(4,1)S(1)} %fusion.34, ...), kind=kOutput, calls=%fused_computation.32 | convolution fusion | flops 1084227584 | bytes 18120712 | tf_op jit(solution)/shard_map/while/body/eval_jaxpr/cond/branch_1_fun/hgqk,khd->hgqd/dot_general | solution.py:68
  116.4 14.5 %conditional.5 = ((f32[4,2,512]{2,1,0:T(2,128)}, f32[4,2,512]{2,1,0:T(2,128)S(1)}, f32[4,2,512,256]{3,2,1,0:T(8,128)})) conditional(s32[]{:T(128)} %convert_element_type.48, (f32[4,2,512]{2,1,0:T(2,128)}, f32[4,2,512]{2,1,0:T(2,128)S(1)}, f32[4,2,512,256]{3,2,1,0:T(8,128)}) %tuple.88, (s32[]{:T(128)}, s32[]{:T(128)}, s32[512]{0:T(512)S(1)}, ...), branch_computations={%region_6.6_spmd, %region_7.9_spmd} | conditional | flops 2174495232 | bytes 39076968 | solution.py:76
  117.6 3.5 %fusion.17 = (f32[4,2,512]{2,1,0:T(2,128)S(1)}, f32[4,512,512,2]{2,1,3,0:T(8,128)S(1)}) fusion(pred[512,512]{0,1:T(8,128)(4,1)S(1)} %fusion.34, bf16[512,4,2,256]{3,0,2,1:T(8,128)(2,1)} %get-tuple-element.457, bf16[2,4096,4,256]{3,1,2,0:T(8,128)(2,1)} %get-tuple-element.456, s32[]{:T(128)S(6)} %select_n.38), kind=kOutput, calls=%fused_computation.26 | convolution fusion | flops 1080029184 | bytes 11812868 | tf_op jit(solution)/shard_map/while/body/eval_jaxpr/cond/branch_1_fun/qhgd,khd->hgqk/dot_general | solution.py:47
  121.0 0.7 max.4
  121.8 1.7 fusion.21
  124.2 6.1 %multiply_add_fusion = f32[4,2,512,256]{3,2,1,0:T(8,128)} fusion(f32[4,2,512,256]{3,2,1,0:T(8,128)} %get-tuple-element.459, f32[4,2,512]{2,1,0:T(2,128)S(1)} %bitcast.69, f32[4,512,512,2]{2,1,3,0:T(8,128)S(1)} %get-tuple-element.549, f32[4,2,512]{2,1,0:T(2,128)S(1)} %max.4, pred[512,512]{0,1:T(8,128)(4,1)S(1)} %fusion.34, ...), kind=kOutput, calls=%fused_computation.32 | convolution fusion | flops 1084227584 | bytes 18120712 | tf_op jit(solution)/shard_map/while/body/eval_jaxpr/cond/branch_1_fun/hgqk,khd->hgqd/dot_general | solution.py:68
  131.6 14.5 %conditional.5 = ((f32[4,2,512]{2,1,0:T(2,128)}, f32[4,2,512]{2,1,0:T(2,128)S(1)}, f32[4,2,512,256]{3,2,1,0:T(8,128)})) conditional(s32[]{:T(128)} %convert_element_type.48, (f32[4,2,512]{2,1,0:T(2,128)}, f32[4,2,512]{2,1,0:T(2,128)S(1)}, f32[4,2,512,256]{3,2,1,0:T(8,128)}) %tuple.88, (s32[]{:T(128)}, s32[]{:T(128)}, s32[512]{0:T(512)S(1)}, ...), branch_computations={%region_6.6_spmd, %region_7.9_spmd} | conditional | flops 2174495232 | bytes 39076968 | solution.py:76
  132.7 3.5 %fusion.17 = (f32[4,2,512]{2,1,0:T(2,128)S(1)}, f32[4,512,512,2]{2,1,3,0:T(8,128)S(1)}) fusion(pred[512,512]{0,1:T(8,128)(4,1)S(1)} %fusion.34, bf16[512,4,2,256]{3,0,2,1:T(8,128)(2,1)} %get-tuple-element.457, bf16[2,4096,4,256]{3,1,2,0:T(8,128)(2,1)} %get-tuple-element.456, s32[]{:T(128)S(6)} %select_n.38), kind=kOutput, calls=%fused_computation.26 | convolution fusion | flops 1080029184 | bytes 11812868 | tf_op jit(solution)/shard_map/while/body/eval_jaxpr/cond/branch_1_fun/qhgd,khd->hgqk/dot_general | solution.py:47
  136.2 0.7 max.4
  136.9 1.7 fusion.21
  139.4 6.1 %multiply_add_fusion = f32[4,2,512,256]{3,2,1,0:T(8,128)} fusion(f32[4,2,512,256]{3,2,1,0:T(8,128)} %get-tuple-element.459, f32[4,2,512]{2,1,0:T(2,128)S(1)} %bitcast.69, f32[4,512,512,2]{2,1,3,0:T(8,128)S(1)} %get-tuple-element.549, f32[4,2,512]{2,1,0:T(2,128)S(1)} %max.4, pred[512,512]{0,1:T(8,128)(4,1)S(1)} %fusion.34, ...), kind=kOutput, calls=%fused_computation.32 | convolution fusion | flops 1084227584 | bytes 18120712 | tf_op jit(solution)/shard_map/while/body/eval_jaxpr/cond/branch_1_fun/hgqk,khd->hgqd/dot_general | solution.py:68
  146.8 14.5 %conditional.5 = ((f32[4,2,512]{2,1,0:T(2,128)}, f32[4,2,512]{2,1,0:T(2,128)S(1)}, f32[4,2,512,256]{3,2,1,0:T(8,128)})) conditional(s32[]{:T(128)} %convert_element_type.48, (f32[4,2,512]{2,1,0:T(2,128)}, f32[4,2,512]{2,1,0:T(2,128)S(1)}, f32[4,2,512,256]{3,2,1,0:T(8,128)}) %tuple.88, (s32[]{:T(128)}, s32[]{:T(128)}, s32[512]{0:T(512)S(1)}, ...), branch_computations={%region_6.6_spmd, %region_7.9_spmd} | conditional | flops 2174495232 | bytes 39076968 | solution.py:76
  147.9 3.5 %fusion.17 = (f32[4,2,512]{2,1,0:T(2,128)S(1)}, f32[4,512,512,2]{2,1,3,0:T(8,128)S(1)}) fusion(pred[512,512]{0,1:T(8,128)(4,1)S(1)} %fusion.34, bf16[512,4,2,256]{3,0,2,1:T(8,128)(2,1)} %get-tuple-element.457, bf16[2,4096,4,256]{3,1,2,0:T(8,128)(2,1)} %get-tuple-element.456, s32[]{:T(128)S(6)} %select_n.38), kind=kOutput, calls=%fused_computation.26 | convolution fusion | flops 1080029184 | bytes 11812868 | tf_op jit(solution)/shard_map/while/body/eval_jaxpr/cond/branch_1_fun/qhgd,khd->hgqk/dot_general | solution.py:47
  152.1 1.7 fusion.21
  154.6 6.1 %multiply_add_fusion = f32[4,2,512,256]{3,2,1,0:T(8,128)} fusion(f32[4,2,512,256]{3,2,1,0:T(8,128)} %get-tuple-element.459, f32[4,2,512]{2,1,0:T(2,128)S(1)} %bitcast.69, f32[4,512,512,2]{2,1,3,0:T(8,128)S(1)} %get-tuple-element.549, f32[4,2,512]{2,1,0:T(2,128)S(1)} %max.4, pred[512,512]{0,1:T(8,128)(4,1)S(1)} %fusion.34, ...), kind=kOutput, calls=%fused_computation.32 | convolution fusion | flops 1084227584 | bytes 18120712 | tf_op jit(solution)/shard_map/while/body/eval_jaxpr/cond/branch_1_fun/hgqk,khd->hgqd/dot_general | solution.py:68
  161.9 14.5 %conditional.5 = ((f32[4,2,512]{2,1,0:T(2,128)}, f32[4,2,512]{2,1,0:T(2,128)S(1)}, f32[4,2,512,256]{3,2,1,0:T(8,128)})) conditional(s32[]{:T(128)} %convert_element_type.48, (f32[4,2,512]{2,1,0:T(2,128)}, f32[4,2,512]{2,1,0:T(2,128)S(1)}, f32[4,2,512,256]{3,2,1,0:T(8,128)}) %tuple.88, (s32[]{:T(128)}, s32[]{:T(128)}, s32[512]{0:T(512)S(1)}, ...), branch_computations={%region_6.6_spmd, %region_7.9_spmd} | conditional | flops 2174495232 | bytes 39076968 | solution.py:76
  163.0 3.5 %fusion.17 = (f32[4,2,512]{2,1,0:T(2,128)S(1)}, f32[4,512,512,2]{2,1,3,0:T(8,128)S(1)}) fusion(pred[512,512]{0,1:T(8,128)(4,1)S(1)} %fusion.34, bf16[512,4,2,256]{3,0,2,1:T(8,128)(2,1)} %get-tuple-element.457, bf16[2,4096,4,256]{3,1,2,0:T(8,128)(2,1)} %get-tuple-element.456, s32[]{:T(128)S(6)} %select_n.38), kind=kOutput, calls=%fused_computation.26 | convolution fusion | flops 1080029184 | bytes 11812868 | tf_op jit(solution)/shard_map/while/body/eval_jaxpr/cond/branch_1_fun/qhgd,khd->hgqk/dot_general | solution.py:47
  167.2 1.7 fusion.21
  169.7 6.1 %multiply_add_fusion = f32[4,2,512,256]{3,2,1,0:T(8,128)} fusion(f32[4,2,512,256]{3,2,1,0:T(8,128)} %get-tuple-element.459, f32[4,2,512]{2,1,0:T(2,128)S(1)} %bitcast.69, f32[4,512,512,2]{2,1,3,0:T(8,128)S(1)} %get-tuple-element.549, f32[4,2,512]{2,1,0:T(2,128)S(1)} %max.4, pred[512,512]{0,1:T(8,128)(4,1)S(1)} %fusion.34, ...), kind=kOutput, calls=%fused_computation.32 | convolution fusion | flops 1084227584 | bytes 18120712 | tf_op jit(solution)/shard_map/while/body/eval_jaxpr/cond/branch_1_fun/hgqk,khd->hgqd/dot_general | solution.py:68
  177.1 14.5 %conditional.5 = ((f32[4,2,512]{2,1,0:T(2,128)}, f32[4,2,512]{2,1,0:T(2,128)S(1)}, f32[4,2,512,256]{3,2,1,0:T(8,128)})) conditional(s32[]{:T(128)} %convert_element_type.48, (f32[4,2,512]{2,1,0:T(2,128)}, f32[4,2,512]{2,1,0:T(2,128)S(1)}, f32[4,2,512,256]{3,2,1,0:T(8,128)}) %tuple.88, (s32[]{:T(128)}, s32[]{:T(128)}, s32[512]{0:T(512)S(1)}, ...), branch_computations={%region_6.6_spmd, %region_7.9_spmd} | conditional | flops 2174495232 | bytes 39076968 | solution.py:76
  178.2 3.5 %fusion.17 = (f32[4,2,512]{2,1,0:T(2,128)S(1)}, f32[4,512,512,2]{2,1,3,0:T(8,128)S(1)}) fusion(pred[512,512]{0,1:T(8,128)(4,1)S(1)} %fusion.34, bf16[512,4,2,256]{3,0,2,1:T(8,128)(2,1)} %get-tuple-element.457, bf16[2,4096,4,256]{3,1,2,0:T(8,128)(2,1)} %get-tuple-element.456, s32[]{:T(128)S(6)} %select_n.38), kind=kOutput, calls=%fused_computation.26 | convolution fusion | flops 1080029184 | bytes 11812868 | tf_op jit(solution)/shard_map/while/body/eval_jaxpr/cond/branch_1_fun/qhgd,khd->hgqk/dot_general | solution.py:47
  181.7 0.7 max.4
  182.4 1.7 fusion.21
  184.9 6.1 %multiply_add_fusion = f32[4,2,512,256]{3,2,1,0:T(8,128)} fusion(f32[4,2,512,256]{3,2,1,0:T(8,128)} %get-tuple-element.459, f32[4,2,512]{2,1,0:T(2,128)S(1)} %bitcast.69, f32[4,512,512,2]{2,1,3,0:T(8,128)S(1)} %get-tuple-element.549, f32[4,2,512]{2,1,0:T(2,128)S(1)} %max.4, pred[512,512]{0,1:T(8,128)(4,1)S(1)} %fusion.34, ...), kind=kOutput, calls=%fused_computation.32 | convolution fusion | flops 1084227584 | bytes 18120712 | tf_op jit(solution)/shard_map/while/body/eval_jaxpr/cond/branch_1_fun/hgqk,khd->hgqd/dot_general | solution.py:68
  192.2 14.5 %conditional.5 = ((f32[4,2,512]{2,1,0:T(2,128)}, f32[4,2,512]{2,1,0:T(2,128)S(1)}, f32[4,2,512,256]{3,2,1,0:T(8,128)})) conditional(s32[]{:T(128)} %convert_element_type.48, (f32[4,2,512]{2,1,0:T(2,128)}, f32[4,2,512]{2,1,0:T(2,128)S(1)}, f32[4,2,512,256]{3,2,1,0:T(8,128)}) %tuple.88, (s32[]{:T(128)}, s32[]{:T(128)}, s32[512]{0:T(512)S(1)}, ...), branch_computations={%region_6.6_spmd, %region_7.9_spmd} | conditional | flops 2174495232 | bytes 39076968 | solution.py:76
  193.4 3.5 %fusion.17 = (f32[4,2,512]{2,1,0:T(2,128)S(1)}, f32[4,512,512,2]{2,1,3,0:T(8,128)S(1)}) fusion(pred[512,512]{0,1:T(8,128)(4,1)S(1)} %fusion.34, bf16[512,4,2,256]{3,0,2,1:T(8,128)(2,1)} %get-tuple-element.457, bf16[2,4096,4,256]{3,1,2,0:T(8,128)(2,1)} %get-tuple-element.456, s32[]{:T(128)S(6)} %select_n.38), kind=kOutput, calls=%fused_computation.26 | convolution fusion | flops 1080029184 | bytes 11812868 | tf_op jit(solution)/shard_map/while/body/eval_jaxpr/cond/branch_1_fun/qhgd,khd->hgqk/dot_general | solution.py:47
  197.6 1.7 fusion.21
  200.0 6.1 %multiply_add_fusion = f32[4,2,512,256]{3,2,1,0:T(8,128)} fusion(f32[4,2,512,256]{3,2,1,0:T(8,128)} %get-tuple-element.459, f32[4,2,512]{2,1,0:T(2,128)S(1)} %bitcast.69, f32[4,512,512,2]{2,1,3,0:T(8,128)S(1)} %get-tuple-element.549, f32[4,2,512]{2,1,0:T(2,128)S(1)} %max.4, pred[512,512]{0,1:T(8,128)(4,1)S(1)} %fusion.34, ...), kind=kOutput, calls=%fused_computation.32 | convolution fusion | flops 1084227584 | bytes 18120712 | tf_op jit(solution)/shard_map/while/body/eval_jaxpr/cond/branch_1_fun/hgqk,khd->hgqd/dot_general | solution.py:68
  207.4 14.5 %conditional.5 = ((f32[4,2,512]{2,1,0:T(2,128)}, f32[4,2,512]{2,1,0:T(2,128)S(1)}, f32[4,2,512,256]{3,2,1,0:T(8,128)})) conditional(s32[]{:T(128)} %convert_element_type.48, (f32[4,2,512]{2,1,0:T(2,128)}, f32[4,2,512]{2,1,0:T(2,128)S(1)}, f32[4,2,512,256]{3,2,1,0:T(8,128)}) %tuple.88, (s32[]{:T(128)}, s32[]{:T(128)}, s32[512]{0:T(512)S(1)}, ...), branch_computations={%region_6.6_spmd, %region_7.9_spmd} | conditional | flops 2174495232 | bytes 39076968 | solution.py:76
  208.5 3.5 %fusion.17 = (f32[4,2,512]{2,1,0:T(2,128)S(1)}, f32[4,512,512,2]{2,1,3,0:T(8,128)S(1)}) fusion(pred[512,512]{0,1:T(8,128)(4,1)S(1)} %fusion.34, bf16[512,4,2,256]{3,0,2,1:T(8,128)(2,1)} %get-tuple-element.457, bf16[2,4096,4,256]{3,1,2,0:T(8,128)(2,1)} %get-tuple-element.456, s32[]{:T(128)S(6)} %select_n.38), kind=kOutput, calls=%fused_computation.26 | convolution fusion | flops 1080029184 | bytes 11812868 | tf_op jit(solution)/shard_map/while/body/eval_jaxpr/cond/branch_1_fun/qhgd,khd->hgqk/dot_general | solution.py:47
  212.7 1.7 fusion.21
  215.2 6.1 %multiply_add_fusion = f32[4,2,512,256]{3,2,1,0:T(8,128)} fusion(f32[4,2,512,256]{3,2,1,0:T(8,128)} %get-tuple-element.459, f32[4,2,512]{2,1,0:T(2,128)S(1)} %bitcast.69, f32[4,512,512,2]{2,1,3,0:T(8,128)S(1)} %get-tuple-element.549, f32[4,2,512]{2,1,0:T(2,128)S(1)} %max.4, pred[512,512]{0,1:T(8,128)(4,1)S(1)} %fusion.34, ...), kind=kOutput, calls=%fused_computation.32 | convolution fusion | flops 1084227584 | bytes 18120712 | tf_op jit(solution)/shard_map/while/body/eval_jaxpr/cond/branch_1_fun/hgqk,khd->hgqd/dot_general | solution.py:68
  221.9 2.6 %select_convert_fusion = bf16[4,2,512,256]{3,2,1,0:T(8,128)(2,1)S(1)} fusion(f32[4,2,512,256]{3,2,1,0:T(8,128)} %get-tuple-element.483, f32[4,2,512]{2,1,0:T(2,128)S(1)} %broadcast_select_fusion, pred[512]{0:T(512)(128)(4,1)S(1)} %broadcast_compare_fusion.5), kind=kLoop, calls=%fused_computation.57 | loop fusion | flops 3145728 | bytes 6308352 | tf_op jit(solution)/shard_map/convert_element_type | solution.py:99
  224.5 2.5 %copy.15 = bf16[512,8,256]{2,1,0:T(8,128)(2,1)} copy(bf16[512,8,256]{2,0,1:T(8,128)(2,1)S(1)} %bitcast.66) | data formatting | bytes 4194304 | tf_op jit(solution)/shard_map/convert_element_type | solution.py:99
  (64 shorter events, 25.0 us)
Async XLA Ops:
  6.5 94.1 %all-gather.2.cloned.1.call-start = ((), (), s32[]{:S(2)}) async-start(), calls=%async_computation | async-start | bytes 18874368 | tf_op jit(solution)/shard_map/all_gather | solution.py:86
Sparse Core Ops, SparseCore 0:
  10.0 90.5 all-gather.1
where the time goes:
time: 236 us; the launch traced here: 234 us
  matrix products  81.8 us (35%)
  waiting for transfers between devices  54.7 us (23%)
  other arithmetic  41.9 us (18%)
  blocking collectives  23 us (10%)
  between operations  14.1 us (6%)
  local copies, waits for them, and re-layouts  12.5 us (5%)
  loops' own time  5.89 us (2%)
    all_gather x1, waiting for transfers between devices, shards(): shard_piece = lax.all_gather(own_pair, 'seq', axis=1, tiled=True)  54.7 us
    dot_general x9, matrix products, compute(): jnp.einsum('hgqk,khd->hgqd', weights.astype(jnp.bfloat16), kv_block[1], p...  51.9 us
    dot_general x9, matrix products, compute(): jnp.einsum('qhgd,khd->hgqk', grouped, kv_block[0], preferred_element_type...  29.9 us
    psum x1, blocking collectives, spread(): return lax.psum(kept, axis)  23 us
    reduce_sum x9, other arithmetic, compute(): totals = totals * rescale + jnp.sum(weights, axis=-1)  14.7 us
    add x9, other arithmetic, compute(): totals = totals * rescale + jnp.sum(weights, axis=-1)  6.6 us
    lt x9, other arithmetic, compute(): visible = visible & (query_pos[:, None] < length_now)  5.88 us
    max x8, other arithmetic, compute(): newest = jnp.maximum(maximum, jnp.max(masked, axis=-1))  5.86 us
  transfers between devices with their start and end apart: 1, of which 1 were waited for; matrix products, arithmetic and copies ran while one was open for 5% of the time, Pallas kernels for 0%

commit v1 on v0

--- a/solution.py
+++ b/solution.py
@@ -6,6 +6,16 @@
 
 WINDOW = 4096
 SINKS = 4
+
+
+def pass_along(x, axis, dim):
+    peers = lax.axis_size(axis)
+    block, tiles = (x, [x])
+    for _ in range(peers - 1):
+        block = lax.ppermute(block, axis, [(i, (i + 1) % peers) for i in range(peers)])
+        tiles.insert(0, block)
+    row_of_blocks = jnp.concatenate(tiles, axis=dim)
+    return jnp.roll(row_of_blocks, (lax.axis_index(axis) + 1) * x.shape[dim], axis=dim)
 
 
 def spread(value, axis, source):
@@ -83,7 +93,7 @@
     own_pair = jnp.stack([key_heads, projected_value_heads])
     sink_pair = spread(own_pair[:, :SINKS], "seq", 0)
     running = attend(running, sink_pair, jnp.int32(0), True)
-    shard_piece = lax.all_gather(own_pair, "seq", axis=1, tiled=True)
+    shard_piece = pass_along(own_pair, "seq", 1)
     piece_rows = shard_piece.shape[1]
     block_size = math.gcd(piece_rows, tok_rows)
 

time: 236 us -> 410 us (1.74)
  waiting for transfers between devices: 54.7 us -> 138 us
  local copies, waits for them, and re-layouts: 12.5 us -> 60.5 us
  matrix products: 81.8 us -> 103 us
  starting transfers between devices: 0.01 us -> 20.4 us
  blocking collectives: 23 us -> 36.6 us
  between operations: 14.1 us -> 0.93 us
    ppermute x0 -> x7, waiting for transfers between devices: none -> 138 us  [pass_along(): lax.ppermute(block, axis, [(i, (i + 1) % peers) for i in range(peers)])]
    all_gather x1 -> x0, waiting for transfers between devices: 54.7 us -> none  [shards(): shard_piece = lax.all_gather(own_pair, 'seq', axis=1, tiled=True)]
    dot_general x9, matrix products: 51.9 us -> 78.7 us  [compute(): jnp.einsum('hgqk,khd->hgqd', weights.astype(jnp.bfloat16), kv_block[1], p...]
    unnamed x1 -> x33, local copies, waits for them, and re-layouts: 3.34 us -> 25.2 us
    ppermute x0 -> x7, starting transfers between devices: none -> 20.4 us  [pass_along(): lax.ppermute(block, axis, [(i, (i + 1) % peers) for i in range(peers)])]
    cond x8 -> x24, local copies, waits for them, and re-layouts: 4.78 us -> 24.4 us
    psum x1, blocking collectives: 23 us -> 36.6 us  [spread(): return lax.psum(kept, axis)]
    dynamic_slice x0 -> x1, local copies, waits for them, and re-layouts: none -> 6.54 us  [pass_along(): jnp.roll(row_of_blocks, (lax.axis_index(axis) + 1) * x.shape[dim], axis=dim)]
  transfers between devices with their start and end apart: 1 -> 7, of which waited for: 1 -> 6; matrix products, arithmetic and copies ran while one was open for 5% -> 3% of each run, Pallas kernels for 0% -> 0%
where the time goes in v1:
time: 410 us; the launch traced here: 407 us
  waiting for transfers between devices  138 us (34%)
  matrix products  103 us (25%)
  local copies, waits for them, and re-layouts  60.5 us (15%)
  other arithmetic  41.3 us (10%)
  blocking collectives  36.6 us (9%)
  starting transfers between devices  20.4 us (5%)
  loops' own time  6.17 us (2%)
    ppermute x7, waiting for transfers between devices, pass_along(): lax.ppermute(block, axis, [(i, (i + 1) % peers) for i in range(peers)])  138 us
    dot_general x9, matrix products, compute(): jnp.einsum('hgqk,khd->hgqd', weights.astype(jnp.bfloat16), kv_block[1], p...  78.7 us
    psum x1, blocking collectives, spread(): return lax.psum(kept, axis)  36.6 us
    unnamed x33, local copies, waits for them, and re-layouts  25.2 us
    cond x24, local copies, waits for them, and re-layouts  24.4 us
    dot_general x9, matrix products, compute(): jnp.einsum('qhgd,khd->hgqk', grouped, kv_block[0], preferred_element_type...  24.3 us
    ppermute x7, starting transfers between devices, pass_along(): lax.ppermute(block, axis, [(i, (i + 1) % peers) for i in range(peers)])  20.4 us
    reduce_sum x9, other arithmetic, compute(): totals = totals * rescale + jnp.sum(weights, axis=-1)  14.9 us
  transfers between devices with their start and end apart: 7, of which 6 were waited for; matrix products, arithmetic and copies ran while one was open for 3% of the time, Pallas kernels for 0%

profile of v1, /device:TPU:7, one launch (start us, length us, event | category | flops | bytes accessed | tf_op | source)
XLA Modules:
  0.0 406.7 jit_solution(1135281862366831605)
XLA Ops:
  2.1 23.0 %collective-permute-done = bf16[2,512,4,256]{3,1,2,0:T(8,128)(2,1)S(1)} collective-permute-done((bf16[2,512,4,256]{3,1,2,0:T(8,128)(2,1)S(1)}, bf16[2,512,4,256]{3,1,2,0:T(8,128)(2,1)S(1)}, u32[]{:S(2)}, u32[]{:S(2)}) %collective-permute-start) | collective-permute-done | bytes 2097184 | tf_op jit(solution)/shard_map/ppermute | solution.py:15
  26.4 3.4 collective-permute-start.1
  29.8 23.0 %collective-permute-done.1 = bf16[2,512,4,256]{3,1,2,0:T(8,128)(2,1)S(1)} collective-permute-done((bf16[2,512,4,256]{3,1,2,0:T(8,128)(2,1)S(1)}, bf16[2,512,4,256]{3,1,2,0:T(8,128)(2,1)S(1)}, u32[]{:S(2)}, u32[]{:S(2)}) %collective-permute-start.1) | collective-permute-done | bytes 2097184 | tf_op jit(solution)/shard_map/ppermute | solution.py:15
  54.1 3.4 collective-permute-start.2
  57.5 23.0 %collective-permute-done.2 = bf16[2,512,4,256]{3,1,2,0:T(8,128)(2,1)S(1)} collective-permute-done((bf16[2,512,4,256]{3,1,2,0:T(8,128)(2,1)S(1)}, bf16[2,512,4,256]{3,1,2,0:T(8,128)(2,1)S(1)}, u32[]{:S(2)}, u32[]{:S(2)}) %collective-permute-start.2) | collective-permute-done | bytes 2097184 | tf_op jit(solution)/shard_map/ppermute | solution.py:15
  81.8 3.4 collective-permute-start.3
  85.1 23.0 %collective-permute-done.3 = bf16[2,512,4,256]{3,1,2,0:T(8,128)(2,1)S(1)} collective-permute-done((bf16[2,512,4,256]{3,1,2,0:T(8,128)(2,1)S(1)}, bf16[2,512,4,256]{3,1,2,0:T(8,128)(2,1)S(1)}, u32[]{:S(2)}, u32[]{:S(2)}) %collective-permute-start.3) | collective-permute-done | bytes 2097184 | tf_op jit(solution)/shard_map/ppermute | solution.py:15
  109.5 3.4 collective-permute-start.4
  112.8 23.0 %collective-permute-done.4 = bf16[2,512,4,256]{3,1,2,0:T(8,128)(2,1)S(1)} collective-permute-done((bf16[2,512,4,256]{3,1,2,0:T(8,128)(2,1)S(1)}, bf16[2,512,4,256]{3,1,2,0:T(8,128)(2,1)S(1)}, u32[]{:S(2)}, u32[]{:S(2)}) %collective-permute-start.4) | collective-permute-done | bytes 2097184 | tf_op jit(solution)/shard_map/ppermute | solution.py:15
  137.2 3.4 collective-permute-start.5
  140.5 23.0 %collective-permute-done.5 = bf16[2,512,4,256]{3,1,2,0:T(8,128)(2,1)} collective-permute-done((bf16[2,512,4,256]{3,1,2,0:T(8,128)(2,1)S(1)}, bf16[2,512,4,256]{3,1,2,0:T(8,128)(2,1)}, u32[]{:S(2)}, u32[]{:S(2)}) %collective-permute-start.5) | collective-permute-done | bytes 2097184 | tf_op jit(solution)/shard_map/ppermute | solution.py:15
  163.5 3.5 collective-permute-start.6
  167.0 3.3 copy.8
  171.0 36.6 %psum.7 = bf16[2,4,4,256]{3,1,2,0:T(4,128)(2,1)S(1)} all-reduce(bf16[2,4,4,256]{3,1,2,0:T(4,128)(2,1)S(1)} %fusion.40), channel_id=1, replica_groups=mesh['batch'=4,'seq'=8] {'seq'}, use_global_device_ids=true, to_apply=%region_0.1 | all-reduce | flops 8192 | bytes 32768 | tf_op jit(solution)/shard_map/psum | solution.py:23
  207.6 9.2 %conditional.2 = (f32[4,2,512]{2,1,0:T(2,128)}, f32[4,2,512]{2,1,0:T(2,128)S(1)}, f32[4,2,512,256]{3,2,1,0:T(8,128)}) conditional(s32[]{:T(128)} %convert_element_type.35, () %tuple.61, (s32[512]{0:T(512)S(1)}, s32[4]{0:T(128)S(1)}, s32[]{:T(128)}, s32[4]{0:T(128)S(1)}, bf16[2,4,4,256]{3,1,2,0:T(4,128)(2,1)S(1)}, ...), branch_computations={%region_1.2_spmd, %region_2.5_spmd} | conditional | flops 17998340 | bytes 6698056 | solution.py:86
  211.9 3.2 convolution_add_fusion
  232.6 6.5 %constant_dynamic-slice_fusion = bf16[2,4096,4,256]{3,1,2,0:T(8,128)(2,1)} fusion(bf16[2,8192,4,256]{3,1,2,0:T(8,128)(2,1)S(1)} %constant_dynamic-update-slice_fusion, s32[]{:T(128)S(6)} %select_n.61), kind=kLoop, calls=%fused_computation.84 | loop fusion | bytes 33554436 | tf_op jit(solution)/shard_map/jit(_roll_dynamic)/dynamic_slice | solution.py:18
  239.1 162.5 %while.22 = (s32[]{:T(128)}, f32[4,2,512]{2,1,0:T(2,128)}, f32[4,2,512]{2,1,0:T(2,128)S(1)}, f32[4,2,512,256]{3,2,1,0:T(8,128)}, s32[]{:T(128)}, /*index=5*/s32[...) while((s32[]{:T(128)}, f32[4,2,512]{2,1,0:T(2,128)}, ...), condition=%wide.region_10.11_spmd.clone, body=%wide.region_5.10_spmd.clone.sunk | while | flops 2174495232 | bytes 72633808 | solution.py:104
  239.8 19.6 %conditional.5 = ((f32[4,2,512]{2,1,0:T(2,128)}, f32[4,2,512]{2,1,0:T(2,128)S(1)}, f32[4,2,512,256]{3,2,1,0:T(8,128)})) conditional(s32[]{:T(128)} %convert_element_type.48, (f32[4,2,512]{2,1,0:T(2,128)}, f32[4,2,512]{2,1,0:T(2,128)S(1)}, f32[4,2,512,256]{3,2,1,0:T(8,128)}) %tuple.88, (s32[]{:T(128)}, s32[]{:T(128)}, s32[512]{0:T(512)S(1)}, ...), branch_computations={%region_6.6_spmd, %region_7.9_spmd} | conditional | flops 2174495232 | bytes 72631424 | solution.py:86
  240.9 2.8 fusion.17
  244.4 2.5 copy-done
  249.4 9.4 %multiply_add_fusion = f32[4,2,512,256]{3,2,1,0:T(8,128)} fusion(f32[4,2,512,256]{3,2,1,0:T(8,128)} %get-tuple-element.459, f32[4,2,512]{2,1,0:T(2,128)S(1)} %bitcast.69, f32[4,512,512,2]{2,1,3,0:T(8,128)} %copy-done, f32[4,2,512]{2,1,0:T(2,128)S(1)} %max.4, pred[512,512]{0,1:T(8,128)(4,1)S(1)} %fusion.34, ...), kind=kOutput, calls=%fused_computation.32 | convolution fusion | flops 1084227584 | bytes 18120712 | tf_op jit(solution)/shard_map/while/body/eval_jaxpr/cond/branch_1_fun/hgqk,khd->hgqd/dot_general | solution.py:78
  260.1 19.6 %conditional.5 = ((f32[4,2,512]{2,1,0:T(2,128)}, f32[4,2,512]{2,1,0:T(2,128)S(1)}, f32[4,2,512,256]{3,2,1,0:T(8,128)})) conditional(s32[]{:T(128)} %convert_element_type.48, (f32[4,2,512]{2,1,0:T(2,128)}, f32[4,2,512]{2,1,0:T(2,128)S(1)}, f32[4,2,512,256]{3,2,1,0:T(8,128)}) %tuple.88, (s32[]{:T(128)}, s32[]{:T(128)}, s32[512]{0:T(512)S(1)}, ...), branch_computations={%region_6.6_spmd, %region_7.9_spmd} | conditional | flops 2174495232 | bytes 72631424 | solution.py:86
  261.2 2.8 fusion.17
  264.7 2.5 copy-done
  269.7 9.4 %multiply_add_fusion = f32[4,2,512,256]{3,2,1,0:T(8,128)} fusion(f32[4,2,512,256]{3,2,1,0:T(8,128)} %get-tuple-element.459, f32[4,2,512]{2,1,0:T(2,128)S(1)} %bitcast.69, f32[4,512,512,2]{2,1,3,0:T(8,128)} %copy-done, f32[4,2,512]{2,1,0:T(2,128)S(1)} %max.4, pred[512,512]{0,1:T(8,128)(4,1)S(1)} %fusion.34, ...), kind=kOutput, calls=%fused_computation.32 | convolution fusion | flops 1084227584 | bytes 18120712 | tf_op jit(solution)/shard_map/while/body/eval_jaxpr/cond/branch_1_fun/hgqk,khd->hgqd/dot_general | solution.py:78
  280.4 19.6 %conditional.5 = ((f32[4,2,512]{2,1,0:T(2,128)}, f32[4,2,512]{2,1,0:T(2,128)S(1)}, f32[4,2,512,256]{3,2,1,0:T(8,128)})) conditional(s32[]{:T(128)} %convert_element_type.48, (f32[4,2,512]{2,1,0:T(2,128)}, f32[4,2,512]{2,1,0:T(2,128)S(1)}, f32[4,2,512,256]{3,2,1,0:T(8,128)}) %tuple.88, (s32[]{:T(128)}, s32[]{:T(128)}, s32[512]{0:T(512)S(1)}, ...), branch_computations={%region_6.6_spmd, %region_7.9_spmd} | conditional | flops 2174495232 | bytes 72631424 | solution.py:86
  281.5 2.8 fusion.17
  290.0 9.4 %multiply_add_fusion = f32[4,2,512,256]{3,2,1,0:T(8,128)} fusion(f32[4,2,512,256]{3,2,1,0:T(8,128)} %get-tuple-element.459, f32[4,2,512]{2,1,0:T(2,128)S(1)} %bitcast.69, f32[4,512,512,2]{2,1,3,0:T(8,128)} %copy-done, f32[4,2,512]{2,1,0:T(2,128)S(1)} %max.4, pred[512,512]{0,1:T(8,128)(4,1)S(1)} %fusion.34, ...), kind=kOutput, calls=%fused_computation.32 | convolution fusion | flops 1084227584 | bytes 18120712 | tf_op jit(solution)/shard_map/while/body/eval_jaxpr/cond/branch_1_fun/hgqk,khd->hgqd/dot_general | solution.py:78
  300.7 19.6 %conditional.5 = ((f32[4,2,512]{2,1,0:T(2,128)}, f32[4,2,512]{2,1,0:T(2,128)S(1)}, f32[4,2,512,256]{3,2,1,0:T(8,128)})) conditional(s32[]{:T(128)} %convert_element_type.48, (f32[4,2,512]{2,1,0:T(2,128)}, f32[4,2,512]{2,1,0:T(2,128)S(1)}, f32[4,2,512,256]{3,2,1,0:T(8,128)}) %tuple.88, (s32[]{:T(128)}, s32[]{:T(128)}, s32[512]{0:T(512)S(1)}, ...), branch_computations={%region_6.6_spmd, %region_7.9_spmd} | conditional | flops 2174495232 | bytes 72631424 | solution.py:86
  301.8 2.7 fusion.17
  305.4 2.5 copy-done
  310.3 9.4 %multiply_add_fusion = f32[4,2,512,256]{3,2,1,0:T(8,128)} fusion(f32[4,2,512,256]{3,2,1,0:T(8,128)} %get-tuple-element.459, f32[4,2,512]{2,1,0:T(2,128)S(1)} %bitcast.69, f32[4,512,512,2]{2,1,3,0:T(8,128)} %copy-done, f32[4,2,512]{2,1,0:T(2,128)S(1)} %max.4, pred[512,512]{0,1:T(8,128)(4,1)S(1)} %fusion.34, ...), kind=kOutput, calls=%fused_computation.32 | convolution fusion | flops 1084227584 | bytes 18120712 | tf_op jit(solution)/shard_map/while/body/eval_jaxpr/cond/branch_1_fun/hgqk,khd->hgqd/dot_general | solution.py:78
  321.0 19.6 %conditional.5 = ((f32[4,2,512]{2,1,0:T(2,128)}, f32[4,2,512]{2,1,0:T(2,128)S(1)}, f32[4,2,512,256]{3,2,1,0:T(8,128)})) conditional(s32[]{:T(128)} %convert_element_type.48, (f32[4,2,512]{2,1,0:T(2,128)}, f32[4,2,512]{2,1,0:T(2,128)S(1)}, f32[4,2,512,256]{3,2,1,0:T(8,128)}) %tuple.88, (s32[]{:T(128)}, s32[]{:T(128)}, s32[512]{0:T(512)S(1)}, ...), branch_computations={%region_6.6_spmd, %region_7.9_spmd} | conditional | flops 2174495232 | bytes 72631424 | solution.py:86
  322.1 2.8 fusion.17
  330.6 9.4 %multiply_add_fusion = f32[4,2,512,256]{3,2,1,0:T(8,128)} fusion(f32[4,2,512,256]{3,2,1,0:T(8,128)} %get-tuple-element.459, f32[4,2,512]{2,1,0:T(2,128)S(1)} %bitcast.69, f32[4,512,512,2]{2,1,3,0:T(8,128)} %copy-done, f32[4,2,512]{2,1,0:T(2,128)S(1)} %max.4, pred[512,512]{0,1:T(8,128)(4,1)S(1)} %fusion.34, ...), kind=kOutput, calls=%fused_computation.32 | convolution fusion | flops 1084227584 | bytes 18120712 | tf_op jit(solution)/shard_map/while/body/eval_jaxpr/cond/branch_1_fun/hgqk,khd->hgqd/dot_general | solution.py:78
  341.3 19.6 %conditional.5 = ((f32[4,2,512]{2,1,0:T(2,128)}, f32[4,2,512]{2,1,0:T(2,128)S(1)}, f32[4,2,512,256]{3,2,1,0:T(8,128)})) conditional(s32[]{:T(128)} %convert_element_type.48, (f32[4,2,512]{2,1,0:T(2,128)}, f32[4,2,512]{2,1,0:T(2,128)S(1)}, f32[4,2,512,256]{3,2,1,0:T(8,128)}) %tuple.88, (s32[]{:T(128)}, s32[]{:T(128)}, s32[512]{0:T(512)S(1)}, ...), branch_computations={%region_6.6_spmd, %region_7.9_spmd} | conditional | flops 2174495232 | bytes 72631424 | solution.py:86
  342.4 2.7 fusion.17
  350.9 9.4 %multiply_add_fusion = f32[4,2,512,256]{3,2,1,0:T(8,128)} fusion(f32[4,2,512,256]{3,2,1,0:T(8,128)} %get-tuple-element.459, f32[4,2,512]{2,1,0:T(2,128)S(1)} %bitcast.69, f32[4,512,512,2]{2,1,3,0:T(8,128)} %copy-done, f32[4,2,512]{2,1,0:T(2,128)S(1)} %max.4, pred[512,512]{0,1:T(8,128)(4,1)S(1)} %fusion.34, ...), kind=kOutput, calls=%fused_computation.32 | convolution fusion | flops 1084227584 | bytes 18120712 | tf_op jit(solution)/shard_map/while/body/eval_jaxpr/cond/branch_1_fun/hgqk,khd->hgqd/dot_general | solution.py:78
  361.6 19.6 %conditional.5 = ((f32[4,2,512]{2,1,0:T(2,128)}, f32[4,2,512]{2,1,0:T(2,128)S(1)}, f32[4,2,512,256]{3,2,1,0:T(8,128)})) conditional(s32[]{:T(128)} %convert_element_type.48, (f32[4,2,512]{2,1,0:T(2,128)}, f32[4,2,512]{2,1,0:T(2,128)S(1)}, f32[4,2,512,256]{3,2,1,0:T(8,128)}) %tuple.88, (s32[]{:T(128)}, s32[]{:T(128)}, s32[512]{0:T(512)S(1)}, ...), branch_computations={%region_6.6_spmd, %region_7.9_spmd} | conditional | flops 2174495232 | bytes 72631424 | solution.py:86
  362.8 2.8 fusion.17
  366.3 2.5 copy-done
  371.2 9.4 %multiply_add_fusion = f32[4,2,512,256]{3,2,1,0:T(8,128)} fusion(f32[4,2,512,256]{3,2,1,0:T(8,128)} %get-tuple-element.459, f32[4,2,512]{2,1,0:T(2,128)S(1)} %bitcast.69, f32[4,512,512,2]{2,1,3,0:T(8,128)} %copy-done, f32[4,2,512]{2,1,0:T(2,128)S(1)} %max.4, pred[512,512]{0,1:T(8,128)(4,1)S(1)} %fusion.34, ...), kind=kOutput, calls=%fused_computation.32 | convolution fusion | flops 1084227584 | bytes 18120712 | tf_op jit(solution)/shard_map/while/body/eval_jaxpr/cond/branch_1_fun/hgqk,khd->hgqd/dot_general | solution.py:78
  381.9 19.6 %conditional.5 = ((f32[4,2,512]{2,1,0:T(2,128)}, f32[4,2,512]{2,1,0:T(2,128)S(1)}, f32[4,2,512,256]{3,2,1,0:T(8,128)})) conditional(s32[]{:T(128)} %convert_element_type.48, (f32[4,2,512]{2,1,0:T(2,128)}, f32[4,2,512]{2,1,0:T(2,128)S(1)}, f32[4,2,512,256]{3,2,1,0:T(8,128)}) %tuple.88, (s32[]{:T(128)}, s32[]{:T(128)}, s32[512]{0:T(512)S(1)}, ...), branch_computations={%region_6.6_spmd, %region_7.9_spmd} | conditional | flops 2174495232 | bytes 72631424 | solution.py:86
  383.1 2.7 fusion.17
  391.5 9.4 %multiply_add_fusion = f32[4,2,512,256]{3,2,1,0:T(8,128)} fusion(f32[4,2,512,256]{3,2,1,0:T(8,128)} %get-tuple-element.459, f32[4,2,512]{2,1,0:T(2,128)S(1)} %bitcast.69, f32[4,512,512,2]{2,1,3,0:T(8,128)} %copy-done, f32[4,2,512]{2,1,0:T(2,128)S(1)} %max.4, pred[512,512]{0,1:T(8,128)(4,1)S(1)} %fusion.34, ...), kind=kOutput, calls=%fused_computation.32 | convolution fusion | flops 1084227584 | bytes 18120712 | tf_op jit(solution)/shard_map/while/body/eval_jaxpr/cond/branch_1_fun/hgqk,khd->hgqd/dot_general | solution.py:78
  401.6 2.6 select_convert_fusion
  404.2 2.5 copy.15
  (126 shorter events, 79.3 us)
Async XLA Ops:
  2.0 23.0 %collective-permute-start = (bf16[2,512,4,256]{3,1,2,0:T(8,128)(2,1)S(1)}, bf16[2,512,4,256]{3,1,2,0:T(8,128)(2,1)S(1)}, u32[]{:S(2)}, u32[]{:S(2)}) collective-permute-start(bf16[2,512,4,256]{3,1,2,0:T(8,128)(2,1)S(1)} %pad_maximum_fusion), channel_id=1, source_target_pairs={{0,1},{1,2},{2,3},{3,4},{4,5},{5,6},{6,7},{7,0},{8,9},{9,10},{10,1... | collective-permute-start | bytes 6291464 | tf_op jit(solution)/shard_map/ppermute | solution.py:15
  25.1 1.3 copy-start.2
  26.4 26.4 %collective-permute-start.1 = (bf16[2,512,4,256]{3,1,2,0:T(8,128)(2,1)S(1)}, bf16[2,512,4,256]{3,1,2,0:T(8,128)(2,1)S(1)}, u32[]{:S(2)}, u32[]{:S(2)}) collective-permute-start(bf16[2,512,4,256]{3,1,2,0:T(8,128)(2,1)S(1)} %collective-permute-done), channel_id=1, source_target_pairs={{0,1},{1,2},{2,3},{3,4},{4,5},{5,6},{6,7},{7,0},{8,9},{9,10},{10,1... | collective-permute-start | bytes 6291464 | tf_op jit(solution)/shard_map/ppermute | solution.py:15
  52.7 1.3 copy-start.4
  54.1 26.4 %collective-permute-start.2 = (bf16[2,512,4,256]{3,1,2,0:T(8,128)(2,1)S(1)}, bf16[2,512,4,256]{3,1,2,0:T(8,128)(2,1)S(1)}, u32[]{:S(2)}, u32[]{:S(2)}) collective-permute-start(bf16[2,512,4,256]{3,1,2,0:T(8,128)(2,1)S(1)} %collective-permute-done.1), channel_id=1, source_target_pairs={{0,1},{1,2},{2,3},{3,4},{4,5},{5,6},{6,7},{7,0},{8,9},{9,10},{10,1... | collective-permute-start | bytes 6291464 | tf_op jit(solution)/shard_map/ppermute | solution.py:15
  80.4 1.3 copy-start.6
  81.8 26.4 %collective-permute-start.3 = (bf16[2,512,4,256]{3,1,2,0:T(8,128)(2,1)S(1)}, bf16[2,512,4,256]{3,1,2,0:T(8,128)(2,1)S(1)}, u32[]{:S(2)}, u32[]{:S(2)}) collective-permute-start(bf16[2,512,4,256]{3,1,2,0:T(8,128)(2,1)S(1)} %collective-permute-done.2), channel_id=1, source_target_pairs={{0,1},{1,2},{2,3},{3,4},{4,5},{5,6},{6,7},{7,0},{8,9},{9,10},{10,1... | collective-permute-start | bytes 6291464 | tf_op jit(solution)/shard_map/ppermute | solution.py:15
  108.1 1.3 copy-start.8
  109.5 26.4 %collective-permute-start.4 = (bf16[2,512,4,256]{3,1,2,0:T(8,128)(2,1)S(1)}, bf16[2,512,4,256]{3,1,2,0:T(8,128)(2,1)S(1)}, u32[]{:S(2)}, u32[]{:S(2)}) collective-permute-start(bf16[2,512,4,256]{3,1,2,0:T(8,128)(2,1)S(1)} %collective-permute-done.3), channel_id=1, source_target_pairs={{0,1},{1,2},{2,3},{3,4},{4,5},{5,6},{6,7},{7,0},{8,9},{9,10},{10,1... | collective-permute-start | bytes 6291464 | tf_op jit(solution)/shard_map/ppermute | solution.py:15
  135.8 1.3 copy-start.9
  137.2 26.4 %collective-permute-start.5 = (bf16[2,512,4,256]{3,1,2,0:T(8,128)(2,1)S(1)}, bf16[2,512,4,256]{3,1,2,0:T(8,128)(2,1)}, u32[]{:S(2)}, u32[]{:S(2)}) collective-permute-start(bf16[2,512,4,256]{3,1,2,0:T(8,128)(2,1)S(1)} %collective-permute-done.4), channel_id=1, source_target_pairs={{0,1},{1,2},{2,3},{3,4},{4,5},{5,6},{6,7},{7,0},{8,9},{9,10},{10,1... | collective-permute-start | bytes 6291464 | tf_op jit(solution)/shard_map/ppermute | solution.py:15
  163.5 53.3 %collective-permute-start.6 = (bf16[2,512,4,256]{3,1,2,0:T(8,128)(2,1)}, bf16[2,512,4,256]{3,1,2,0:T(8,128)(2,1)}, u32[]{:S(2)}, u32[]{:S(2)}) collective-permute-start(bf16[2,512,4,256]{3,1,2,0:T(8,128)(2,1)} %collective-permute-done.5), channel_id=1, source_target_pairs={{0,1},{1,2},{2,3},{3,4},{4,5},{5,6},{6,7},{7,0},{8,9},{9,10},{10,1... | collective-permute-start | bytes 6291464 | tf_op jit(solution)/shard_map/ppermute | solution.py:15
  216.9 7.5 %copy-start.7 = (bf16[2,512,4,256]{3,1,2,0:T(8,128)(2,1)S(1)}, bf16[2,512,4,256]{3,1,2,0:T(8,128)(2,1)}, u32[]{:S(2)}) copy-start(bf16[2,512,4,256]{3,1,2,0:T(8,128)(2,1)} %copy-done.6) | copy-start | bytes 6291460
  218.8 5.7 %copy-start.5 = (bf16[2,512,4,256]{3,1,2,0:T(8,128)(2,1)S(1)}, bf16[2,512,4,256]{3,1,2,0:T(8,128)(2,1)}, u32[]{:S(2)}) copy-start(bf16[2,512,4,256]{3,1,2,0:T(8,128)(2,1)} %copy-done.4) | copy-start | bytes 6291460
  220.7 4.0 copy-start.3
  232.5 6.6 %copy-start.1 = (bf16[512,8,256]{2,0,1:T(8,128)(2,1)S(1)}, bf16[512,8,256]{2,0,1:T(8,128)(2,1)}, u32[]{:S(2)}) copy-start(bf16[512,8,256]{2,0,1:T(8,128)(2,1)} %copy.8) | copy-start | bytes 6291460
  243.7 3.2 copy-start
  264.0 3.2 copy-start
  284.3 3.2 copy-start
  304.6 3.2 copy-start
  324.9 3.2 copy-start
  345.2 3.2 copy-start
  365.5 3.2 copy-start
  385.8 3.2 copy-start
